TPU v7x, 32 devices: a whole 2x2x4 slice. The times are simulated.
32 devices in a mesh: groups: 2 (over x), row: 16 (over z, y, core).
Axes of the slice: x: 2, y: 2, z: 4, core: 2. Of those that a mesh axis runs over, the one named last changes fastest.
Arguments:
- orbitals: bfloat16 [4096, 512], P(('groups', 'row')), parts along dimension 0, may hold values from -1.296875 to 1.296875
- basis: bfloat16 [4096, 1024], P(('groups', 'row')), parts along dimension 0, may hold values from -0.1875 to 0.1875
- kernel: bfloat16 [4096, 2048], P(('groups', 'row')), parts along dimension 0, may hold values from -6 to 6
Outputs:
- exchange_matrix: float32 [2048, 1024], P('groups', 'row'), parts along dimension 0
There are 2 independent parts, one for each index of `groups`. A program takes and returns all parts, laid end to end along the dimension named above; each array names one. Nothing has to cross between parts.
All inputs are finite; a program needn't handle non-finite values.
Results may differ from a plain program's by a relative error of at most 0.0041.
Values may be sent and summed in bfloat16 or wider, within the bound.
A program may use at most 128 MiB of HBM per device.

v0:
```python
import functools

import jax
import jax.numpy as jnp
from jax import lax
from jax.experimental import pallas as pl
from jax.experimental.pallas import tpu as pltpu
from jax.sharding import PartitionSpec as P

LANES = 128
LEAD, LEAD_Y, LATE, ACROSS = (0, 7, 7), (0, 7, 7), 0, (2.1, 5.6)
MESH = pl.DeviceIdType.MESH


def layout(mesh):
    n = mesh.shape["row"]
    try:
        line = mesh.devices[0]
        places = [tuple(d.coords) + (d.core_on_chip,) for d in line]
    except AttributeError:
        return n, 1, 1
    cores = len({p[-1] for p in places})
    axes = [a for a in range(3) if len({p[a] for p in places}) > 1]
    sizes = {a: len({p[a] for p in places}) for a in axes}
    for axis_z in axes:
        rest = [a for a in axes if a != axis_z]
        if len(rest) > 1 or (rest and sizes[rest[0]] != 2):
            continue
        y_size = sizes[rest[0]] if rest else 1
        z0 = min(p[axis_z] for p in places)
        y0 = min(p[rest[0]] for p in places) if rest else 0
        found = [
            ((p[axis_z] - z0) * y_size + (p[rest[0]] - y0 if rest else 0)) * cores + p[-1]
            for p in places
        ]
        if found == list(range(n)):
            return sizes[axis_z], y_size, cores
    return n, 1, 1


def kernel(
    dims, o_in, b_in, k_in, out_ref,
    o_all, b_all, k_v, w, app_t, got, in_sem, send_sem, recv_sem, a2a_send, a2a_recv,
):
    Z, Y, C = dims
    n = Z * Y * C
    units = Z * Y
    parts = 3
    rows = o_in.shape[0]
    half_cols = b_all.shape[-1]
    groups = half_cols // LANES
    cw = app_t.shape[0] * app_t.shape[1] // n
    per = LANES // cw

    me = lax.axis_index("row")
    c = me % C
    y = (me // C) % Y
    z = me // (C * Y)
    peer_y = (Y - 1) - y

    def index(zz, yy, cc):
        return (zz * Y + yy) * C + cc

    up_dev = index(jnp.minimum(z + 1, Z - 1), y, c)
    down_dev = index(jnp.maximum(z - 1, 0), y, c)
    y_dev = index(z, peer_y, c)
    sib_dev = index(z, y, (C - 1) - c)
    has_up = z < Z - 1
    has_down = z > 0

    def chunk(i, p):
        return o_all.at[i] if p == 0 else b_all.at[p - 1, i]

    def copy(i, p, kind):
        dev = (up_dev, down_dev, y_dev, sib_dev)[kind]
        return pltpu.make_async_remote_copy(
            src_ref=chunk(i, p),
            dst_ref=chunk(i, p),
            send_sem=send_sem.at[kind, p, i // C],
            recv_sem=recv_sem.at[p, i],
            device_id={"row": dev},
            device_id_type=MESH,
        )

    def wait_recv(i, p):
        copy(i, p, 3).wait_recv()

    loads = [pltpu.make_async_copy(o_in, o_all.at[me], in_sem.at[0])]
    for g in range(2 * groups):
        h, s = g % 2, g // 2
        loads.append(
            pltpu.make_async_copy(
                b_in.at[:, pl.ds(g * LANES, LANES)],
                b_all.at[h, me, :, pl.ds(s * LANES, LANES)],
                in_sem.at[1 + g],
            )
        )
    k_load = pltpu.make_async_copy(k_in, k_v, in_sem.at[1 + 2 * groups])
    for load in loads:
        load.start()
    k_load.start()

    barrier = pltpu.get_barrier_semaphore()

    def greet(dev):
        pl.semaphore_signal(barrier, inc=1, device_id={"row": dev}, device_id_type=MESH)

    pl.when(has_up)(lambda: greet(up_dev))
    pl.when(has_down)(lambda: greet(down_dev))
    if Y > 1:
        greet(y_dev)
    if C > 1:
        greet(sib_dev)
    others = (Y > 1) + (C > 1)
    pl.semaphore_wait(barrier, others + has_up.astype(jnp.int32) + has_down.astype(jnp.int32))

    relays = Y > 1 and Z >= 4
    both, either = jnp.logical_and, jnp.logical_or

    def goes_across(zz, p):
        if not relays:
            return True
        turn = c == p % C
        end = either(both(both(z == 0, zz == 1), turn), both(both(z == Z - 1, zz == Z - 2), turn))
        beside = either(both(z == 1, zz == 0), both(z == Z - 2, zz == Z - 1))
        return jnp.logical_not(either(end, beside))

    def relay_up(p):
        return either(z == 0, both(z == Z - 2, c == p % C))

    def relay_down(p):
        return either(z == Z - 1, both(z == 1, c == p % C))

    def spread(i, zz, p, up=False, down=False, across=False):
        if up:
            pl.when(has_up)(lambda: copy(i, p, 0).start())
        if down:
            pl.when(has_down)(lambda: copy(i, p, 1).start())
        if across and Y > 1:
            pl.when(goes_across(zz, p))(lambda: copy(i, p, 2).start())
        if C > 1:
            copy(i, p, 3).start()

    def own(p):
        if p == 0:
            loads[0].wait()
        else:
            for g in range(2 * groups):
                if g % 2 == p - 1:
                    loads[1 + g].wait()
        pl.when(has_up)(lambda: copy(me, p, 0).start())
        pl.when(has_down)(lambda: copy(me, p, 1).start())
        if C > 1:
            copy(me, p, 3).start()

    def own_across(p):
        copy(me, p, 2).start()

    def along(p, t):
        def low():
            i = index(z - t, y, c)
            wait_recv(i, p)
            spread(i, z - t, p, up=True, across=True)

        def high():
            i = index(z + t, y, c)
            wait_recv(i, p)
            spread(i, z + t, p, down=True, across=True)

        pl.when(z - t >= 0)(low)
        pl.when(z + t < Z)(high)

    def across(p, t):
        def one(zz):
            i = index(zz, peer_y, c)
            wait_recv(i, p)
            if relays and t == 0:
                pl.when(relay_up(p))(lambda: copy(i, p, 0).start())
                pl.when(relay_down(p))(lambda: copy(i, p, 1).start())
            spread(i, zz, p)

        if t == 0:
            one(z)
        else:
            pl.when(z - t >= 0)(lambda: one(z - t))
            pl.when(z + t < Z)(lambda: one(z + t))

    stride = (Z - 0.5) if relays else (Z if Y > 1 else max(Z - 1, 1))
    events = []
    for p in range(parts):
        base = p * stride
        events.append((base - LEAD[p], p, functools.partial(own, p)))
        for t in range(1, Z):
            events.append((base + t + LATE * (t > 1), p, functools.partial(along, p, t)))
        if Y > 1:
            events.append((base - LEAD_Y[p] + 0.01, p, functools.partial(own_across, p)))
            for t in range(Z):
                events.append((base + t + ACROSS[t > 0], p, functools.partial(across, p, t)))
    events.sort(key=lambda e: e[0])
    last = [max(k for k, e in enumerate(events) if e[1] == p) for p in range(parts)]

    def wait_sibling(p, u):
        if C > 1:
            wait_recv(u * C + (C - 1) - c, p)

    def weigh(u):
        if u == 0:
            k_load.wait()
        wait_sibling(0, u)
        cols = pl.ds(u * C * rows, C * rows)
        block = o_all[u * C:(u + 1) * C].reshape(C * rows, o_all.shape[-1])
        density = lax.dot_general(
            o_all[me], block, (((1,), (1,)), ((), ())), preferred_element_type=jnp.float32
        )
        w[:, cols] = (density * k_v[:, cols].astype(jnp.float32)).astype(jnp.bfloat16)

    wide = 2 * LANES if groups % 2 == 0 else LANES
    depth = min(n, max(1, 2048 // rows))

    def apply(h, j):
        if j == 0:
            for u in range(units):
                wait_sibling(1 + h, u)
        cols = pl.ds(j * wide, wide)

        def term(q):
            block = b_all[h, pl.ds(q * depth, depth), :, cols].reshape(depth * rows, wide)
            return jnp.dot(
                w[:, pl.ds(pl.multiple_of(q * depth * rows, LANES), depth * rows)],
                block,
                preferred_element_type=jnp.float32,
            )

        if n == depth:
            total = term(0)
        else:
            total = lax.fori_loop(
                0, n // depth, lambda q, a: a + term(q), jnp.zeros((rows, wide), jnp.float32)
            )
        app_t[h, cols, :] = total.astype(jnp.bfloat16).T

    count = n // 2

    def exchange(h, q):
        qq = (q + me) % count
        s, e = qq // per, qq % per
        d = (2 * s + h) * per + e
        off = pl.multiple_of(s * LANES + e * cw, 16)
        return d, pltpu.make_async_remote_copy(
            src_ref=app_t.at[h, pl.ds(off, cw), :],
            dst_ref=got.at[:, pl.ds(pl.multiple_of(me * rows, LANES), rows)],
            send_sem=a2a_send.at[h, q],
            recv_sem=a2a_recv.at[me],
            device_id={"row": d},
            device_id_type=MESH,
        ), pltpu.make_async_copy(
            app_t.at[h, pl.ds(off, cw), :],
            got.at[:, pl.ds(pl.multiple_of(me * rows, LANES), rows)],
            a2a_recv.at[me],
        )

    def hand_out(h):
        for q in range(count):
            d, remote, local = exchange(h, q)
            pl.when(d != me)(lambda: remote.start())
            pl.when(d == me)(lambda: local.start())

    work = {p: [] for p in range(parts)}
    for u in range(units):
        work[0].append(functools.partial(weigh, u))
    for h in range(2):
        for j in range(half_cols // wide):
            work[1 + h].append(functools.partial(apply, h, j))
        work[1 + h].append(functools.partial(hand_out, h))

    queue = []
    for k, (_, _, event) in enumerate(events):
        event()
        if queue:
            queue.pop(0)()
        for p in range(parts):
            if last[p] == k:
                queue.extend(work[p])
    for item in queue:
        item()

    for src in range(n):
        pltpu.make_async_copy(
            got.at[:, pl.ds(src * rows, rows)], got.at[:, pl.ds(src * rows, rows)], a2a_recv.at[src]
        ).wait()
    for h in range(2):
        for j in range(half_cols // wide):
            cols = pl.ds(j * wide, wide)

            def term(q):
                block = b_all[h, pl.ds(q * depth, depth), :, cols].reshape(depth * rows, wide)
                return jnp.dot(
                    got[:, pl.ds(pl.multiple_of(q * depth * rows, LANES), depth * rows)],
                    block,
                    preferred_element_type=jnp.float32,
                )

            if n == depth:
                total = term(0)
            else:
                total = lax.fori_loop(
                    0, n // depth, lambda q, a: a + term(q), jnp.zeros((cw, wide), jnp.float32)
                )
            for v in range(wide // LANES):
                g = 2 * (j * (wide // LANES) + v) + h
                out_ref[:, pl.ds(g * LANES, LANES)] = total[:, v * LANES:(v + 1) * LANES]

    for h in range(2):
        for q in range(count):
            d, remote, _ = exchange(h, q)
            pl.when(d != me)(lambda: remote.wait_send())
    for p in range(parts):
        for zz in range(Z):
            i = index(zz, y, c)
            pl.when(jnp.logical_and(has_up, zz <= z))(lambda: copy(i, p, 0).wait_send())
            pl.when(jnp.logical_and(has_down, zz >= z))(lambda: copy(i, p, 1).wait_send())
            if Y > 1:
                pl.when(goes_across(zz, p))(lambda: copy(i, p, 2).wait_send())
        if relays:
            i = index(z, peer_y, c)
            pl.when(relay_up(p))(lambda: copy(i, p, 0).wait_send())
            pl.when(relay_down(p))(lambda: copy(i, p, 1).wait_send())
        if C > 1:
            for u in range(units):
                copy(u * C + c, p, 3).wait_send()


def shards(dims, orbitals, basis, kernel_block):
    Z, Y, C = dims
    n = Z * Y * C
    rows, nocc = orbitals.shape
    nb = basis.shape[1]
    points = kernel_block.shape[1]
    half = nb // 2
    cw = nb // n
    bf16 = jnp.bfloat16
    any_space = pl.BlockSpec(memory_space=pl.ANY)
    return pl.pallas_call(
        functools.partial(kernel, dims),
        out_shape=jax.ShapeDtypeStruct((cw, nb), jnp.float32),
        in_specs=[any_space] * 3,
        out_specs=pl.BlockSpec(memory_space=pltpu.VMEM),
        scratch_shapes=[
            pltpu.VMEM((n, rows, nocc), bf16),
            pltpu.VMEM((2, n, rows, half), bf16),
            pltpu.VMEM((rows, points), bf16),
            pltpu.VMEM((rows, points), bf16),
            pltpu.VMEM((2, half, rows), bf16),
            pltpu.VMEM((cw, points), bf16),
            pltpu.SemaphoreType.DMA((2 + nb // LANES,)),
            pltpu.SemaphoreType.DMA((4, 3, Z * Y)),
            pltpu.SemaphoreType.DMA((3, n)),
            pltpu.SemaphoreType.DMA((2, n // 2)),
            pltpu.SemaphoreType.DMA((n,)),
        ],
        compiler_params=pltpu.CompilerParams(
            collective_id=0, has_side_effects=True, vmem_limit_bytes=60 * 1024 * 1024
        ),
    )(orbitals, basis, kernel_block).T


def solution(mesh):
    spec = P(("groups", "row"), None)
    return jax.shard_map(
        functools.partial(shards, layout(mesh)),
        mesh=mesh,
        in_specs=(spec, spec, spec),
        out_specs=P("groups", "row"),
        check_vma=False,
    )
```

profile of v0, /device:TPU:5, one launch (start us, length us, event | category | flops | bytes accessed | tf_op | source)
XLA Modules:
  0.0 50.3 jit_solution(11088506550724070594)
XLA Ops:
  0.0 48.7 %shard_map.37 = f32[64,1024]{1,0:T(8,128)} custom-call(bf16[128,512]{1,0:T(8,128)(2,1)} %o_in.1, bf16[128,1024]{1,0:T(8,128)(2,1)} %b_in.1, bf16[128,2048]{1,0:T(8,128)(2,1)} %k_in.1), custom_call_target="tpu_custom_call" | custom-call | tf_op jit(solution)/shard_map/pallas_call | solution.py:343
  48.7 1.7 %copy.5 = f32[1024,64]{0,1:T(8,128)} copy(f32[1024,64]{0,1:T(8,128)} %bitcast.1) | data formatting | bytes 524288
where the time goes:
time: 50.5 us; the launch traced here: 50.3 us
  Pallas kernels  48.7 us (96%)
  local copies, waits for them, and re-layouts  1.67 us (3%)
    pallas_call x1, Pallas kernels, shards(): pl.pallas_call(functools.partial(kernel, dims), out_shape=jax.ShapeDtypeS...  48.7 us
    unnamed x1, local copies, waits for them, and re-layouts  1.67 us

commit v1 on v0

--- a/solution.py
+++ b/solution.py
@@ -10,6 +10,7 @@
 LANES = 128
 LEAD, LEAD_Y, LATE, ACROSS = (0, 7, 7), (0, 7, 7), 0, (2.1, 5.6)
 MESH = pl.DeviceIdType.MESH
+OPARTS, STEP, HOP, AHEAD, LAZY, MOVED, AGE = 2, 14, 32, 60, 60, 1, 4
 
 
 def layout(mesh):
@@ -330,12 +331,325 @@
                 copy(u * C + c, p, 3).wait_send()
 
 
+def routes(Z, Y, units):
+    parents = {}
+    for zs in range(Z):
+        for ys in range(Y):
+            for u in range(units):
+                tree = {}
+                for z in range(Z):
+                    for y in range(Y):
+                        if (z, y) == (zs, ys):
+                            continue
+                        if y == ys:
+                            tree[z, y] = (z - 1, y) if z > zs else (z + 1, y)
+                        elif (zs, z) in ((0, 1), (Z - 1, Z - 2)):
+                            tree[z, y] = (zs, y)
+                        elif (zs, z) in ((1, 0), (Z - 2, Z - 1)) and u % 2 == MOVED:
+                            tree[z, y] = (zs, y)
+                        else:
+                            tree[z, y] = (z, ys)
+                parents[zs, ys, u] = tree
+    return parents
+
+
+def timetable(Z, Y, units, step, hop):
+    parents = routes(Z, Y, units)
+    kids, height = {}, {}
+    for key, tree in parents.items():
+        children = {}
+        for node, parent in tree.items():
+            children.setdefault(parent, []).append(node)
+
+        def depth(node):
+            return max((1 + depth(child) for child in children.get(node, [])), default=0)
+
+        kids[key] = children
+        height[key] = {node: depth(node) for node in list(tree) + [key[:2]]}
+    tick = 0
+    queued, free, flying, starts, arrival = {}, {}, [], [], {}
+
+    def have(node, key, now):
+        arrival[node, key] = now
+        for child in kids[key].get(node, []):
+            inward = (key[0] - node[0]) * (1 if 2 * node[0] < Z else -1)
+            rank = (key[2], -height[key][child], inward, key[1] == node[1])
+            queued.setdefault((node, child), []).append((rank, key))
+
+    for key in sorted(parents):
+        have(key[:2], key, 0)
+    while flying or any(queued.values()):
+        landed = [f for f in flying if f[0] <= tick]
+        flying = [f for f in flying if f[0] > tick]
+        for _, node, key in landed:
+            have(node, key, tick)
+        for link, waiting in queued.items():
+            if waiting and free.get(link, 0) <= tick:
+                waiting.sort()
+                _, key = waiting.pop(0)
+                starts.append((tick, link, key))
+                free[link] = tick + step
+                flying.append((tick + step + hop, link[1], key))
+        tick += 1
+    return starts, arrival
+
+
+def program(Z, Y, role, units, step, hop, ahead):
+    starts, arrival = timetable(Z, Y, units, step, hop)
+    node = (role, 0)
+    passed = {key for _, link, key in starts if link[0] == node}
+    moves = []
+    for (where, key), when in arrival.items():
+        if where == node and key[:2] != node:
+            moves.append((when + (0 if key in passed else LAZY), 0, "take", key, None))
+    latest = {}
+    for when, (parent, child), key in starts:
+        if parent == node:
+            kind = 2 if child[1] != node[1] else (0 if child[0] > node[0] else 1)
+            at = max(arrival[node, key], when - ahead, latest.get(kind, 0))
+            latest[kind] = at
+            moves.append((at, 1, "send", key, kind))
+    moves.sort(key=lambda move: move[:2])
+    return moves
+
+
+def planned(
+    dims, o_in, b_in, k_in, out_ref,
+    o_all, b_all, k_v, w, app_t, got, in_sem, send_sem, recv_sem, a2a_send, a2a_recv,
+):
+    Z, Y, C = dims
+    n = Z * Y * C
+    rows = o_in.shape[0]
+    blocks, wide = b_all.shape[0], b_all.shape[-1]
+    cw = got.shape[1]
+    owners = wide // cw
+    cut = rows // OPARTS
+    units = OPARTS + blocks
+    order = sorted(range(blocks), key=lambda b: (min(b, blocks - 1 - b), b))
+    roles = (Z + 1) // 2
+
+    me = lax.axis_index("row")
+    c = me % C
+    y = (me // C) % Y
+    z = me // (C * Y)
+    low = 2 * z < Z
+    role = jnp.minimum(z, Z - 1 - z)
+
+    def index(zz, yy, cc):
+        return (zz * Y + yy) * C + cc
+
+    def place(zm):
+        return jnp.where(low, zm, Z - 1 - zm)
+
+    def device(key):
+        return index(place(key[0]), y if key[1] == 0 else (Y - 1) - y, c)
+
+    inner = index(place(jnp.minimum(role + 1, Z - 1)), y, c)
+    outer = index(place(jnp.maximum(role - 1, 0)), y, c)
+    y_dev = index(z, (Y - 1) - y, c)
+    sib_dev = index(z, y, (C - 1) - c)
+
+    def chunk(i, u):
+        if u < OPARTS:
+            return o_all.at[i, pl.ds(u * cut, cut)]
+        return b_all.at[order[u - OPARTS], i]
+
+    def copy(i, u, kind):
+        return pltpu.make_async_remote_copy(
+            src_ref=chunk(i, u),
+            dst_ref=chunk(i, u),
+            send_sem=send_sem.at[kind, u, i // C],
+            recv_sem=recv_sem.at[u, i],
+            device_id={"row": (inner, outer, y_dev, sib_dev)[kind]},
+            device_id_type=MESH,
+        )
+
+    loads = []
+    for u in range(units):
+        if u < OPARTS:
+            source = o_in.at[pl.ds(u * cut, cut)]
+        else:
+            source = b_in.at[:, pl.ds(order[u - OPARTS] * wide, wide)]
+        loads.append(pltpu.make_async_copy(source, chunk(me, u), in_sem.at[u]))
+    k_load = pltpu.make_async_copy(k_in, k_v, in_sem.at[units])
+    for load in loads:
+        load.start()
+    k_load.start()
+
+    barrier = pltpu.get_barrier_semaphore()
+
+    def greet(dev):
+        pl.semaphore_signal(barrier, inc=1, device_id={"row": dev}, device_id_type=MESH)
+
+    greet(inner)
+    pl.when(role > 0)(lambda: greet(outer))
+    greet(y_dev)
+    greet(sib_dev)
+    pl.semaphore_wait(barrier, 3 + (role > 0).astype(jnp.int32))
+
+    def weigh(chip):
+        i = index(place(chip[0]), y if chip[1] == 0 else (Y - 1) - y, 0)
+        span = pl.ds(pl.multiple_of(i * rows, LANES), C * rows)
+        block = o_all[pl.ds(i, C)].reshape(C * rows, o_all.shape[-1])
+        density = lax.dot_general(
+            o_all[me], block, (((1,), (1,)), ((), ())), preferred_element_type=jnp.float32
+        )
+        w[:, span] = (density * k_v[:, span].astype(jnp.float32)).astype(jnp.bfloat16)
+
+    def apply(b):
+        total = jnp.dot(
+            w[...], b_all[b].reshape(n * rows, wide), preferred_element_type=jnp.float32
+        )
+        app_t[b] = total.astype(jnp.bfloat16).T
+
+    def exchange(b, q):
+        e = (q + me) % owners
+        d = b * owners + e
+        source = app_t.at[b, pl.ds(pl.multiple_of(e * cw, 16), cw), :]
+        target = got.at[me]
+        return d, pltpu.make_async_remote_copy(
+            src_ref=source,
+            dst_ref=target,
+            send_sem=a2a_send.at[b, q],
+            recv_sem=a2a_recv.at[me],
+            device_id={"row": d},
+            device_id_type=MESH,
+        ), lambda: pltpu.make_async_copy(source, target, a2a_recv.at[me])
+
+    def hand_out(b):
+        for q in range(owners):
+            d, remote, local = exchange(b, q)
+            pl.when(d != me)(remote.start)
+            pl.when(d == me)(lambda: local().start())
+
+    def from_sibling(key):
+        i = device(key) - c + (C - 1) - c
+        copy(i, key[2], 3).wait_recv()
+
+    def run(moves, own):
+        chips = [(zz, yy) for zz in range(Z) for yy in range(Y)]
+        missing = {u: set(chips) for u in range(units)}
+        seen, weighed, ready, loaded, whole, taken = set(), [], [], set(), {}, [0]
+
+        def arrived(key):
+            missing[key[2]].discard(key[:2])
+            if key[2] < OPARTS and all(key[:2] not in missing[u] for u in range(OPARTS)):
+                ready.append((taken[0], key))
+            if not missing[key[2]]:
+                whole[key[2]] = taken[0]
+
+        def compute(age):
+            for item in [r for r in ready if r[0] + age <= taken[0]]:
+                ready.remove(item)
+                chip = item[1][:2]
+                if not weighed:
+                    k_load.wait()
+                for u in range(OPARTS):
+                    from_sibling(chip + (u,))
+                weigh(chip)
+                weighed.append(chip)
+            for s in range(blocks):
+                u = OPARTS + s
+                if len(weighed) == len(chips) and u in whole and whole[u] + age <= taken[0] and u not in seen:
+                    seen.add(u)
+                    for chip in chips:
+                        from_sibling(chip + (u,))
+                    apply(order[s])
+                    hand_out(order[s])
+
+        for u in range(units):
+            arrived(own + (u,))
+
+        for _, _, move, key, kind in moves:
+            if move == "take":
+                compute(AGE)
+                copy(device(key), key[2], 3).wait_recv()
+                copy(device(key), key[2], 3).start()
+                taken[0] += 1
+                arrived(key)
+            else:
+                if key[:2] == own and key[2] not in loaded:
+                    loaded.add(key[2])
+                    loads[key[2]].wait()
+                    copy(me, key[2], 3).start()
+                copy(device(key), key[2], kind).start()
+        compute(0)
+
+    plans = [program(Z, Y, r, units, STEP, HOP, AHEAD) for r in range(roles)]
+    for r in range(roles):
+        pl.when(role == r)(functools.partial(run, plans[r], (r, 0)))
+
+    for src in range(n):
+        pltpu.make_async_copy(
+            got.at[src], got.at[src], a2a_recv.at[src]
+        ).wait()
+    mine = jnp.concatenate([got[src] for src in range(n)], axis=1)
+    for b in range(blocks):
+        out_ref[:, pl.ds(b * wide, wide)] = jnp.dot(
+            mine, b_all[b].reshape(n * rows, wide), preferred_element_type=jnp.float32
+        )
+
+    for b in range(blocks):
+        for q in range(owners):
+            d, remote, _ = exchange(b, q)
+            pl.when(d != me)(remote.wait_send)
+
+    def drain(moves):
+        for _, _, move, key, kind in moves:
+            if move == "send":
+                copy(device(key), key[2], kind).wait_send()
+
+    for r in range(roles):
+        pl.when(role == r)(functools.partial(drain, plans[r]))
+    for u in range(units):
+        for chip in range(Z * Y):
+            copy(chip * C + c, u, 3).wait_send()
+
+
+def planned_shards(dims, orbitals, basis, kernel_block):
+    Z, Y, C = dims
+    n = Z * Y * C
+    rows, nocc = orbitals.shape
+    nb = basis.shape[1]
+    points = kernel_block.shape[1]
+    wide = nb // Z
+    cw = nb // n
+    units = OPARTS + Z
+    bf16 = jnp.bfloat16
+    any_space = pl.BlockSpec(memory_space=pl.ANY)
+    return pl.pallas_call(
+        functools.partial(planned, dims),
+        out_shape=jax.ShapeDtypeStruct((cw, nb), jnp.float32),
+        in_specs=[any_space] * 3,
+        out_specs=pl.BlockSpec(memory_space=pltpu.VMEM),
+        scratch_shapes=[
+            pltpu.VMEM((n, rows, nocc), bf16),
+            pltpu.VMEM((Z, n, rows, wide), bf16),
+            pltpu.VMEM((rows, points), bf16),
+            pltpu.VMEM((rows, points), bf16),
+            pltpu.VMEM((Z, wide, rows), bf16),
+            pltpu.VMEM((n, cw, rows), bf16),
+            pltpu.SemaphoreType.DMA((units + 1,)),
+            pltpu.SemaphoreType.DMA((4, units, Z * Y)),
+            pltpu.SemaphoreType.DMA((units, n)),
+            pltpu.SemaphoreType.DMA((Z, wide // cw)),
+            pltpu.SemaphoreType.DMA((n,)),
+        ],
+        compiler_params=pltpu.CompilerParams(
+            collective_id=0, has_side_effects=True, vmem_limit_bytes=60 * 1024 * 1024
+        ),
+    )(orbitals, basis, kernel_block).T
+
+
 def shards(dims, orbitals, basis, kernel_block):
     Z, Y, C = dims
     n = Z * Y * C
     rows, nocc = orbitals.shape
     nb = basis.shape[1]
     points = kernel_block.shape[1]
+    whole = nb % (Z * LANES) == 0 and rows % (16 * OPARTS) == 0 and (nb // n) % 16 == 0
+    if Y == 2 and C == 2 and Z // 2 == 2 and whole:
+        return planned_shards(dims, orbitals, basis, kernel_block)
     half = nb // 2
     cw = nb // n
     bf16 = jnp.bfloat16

time: 50.5 us -> 48.1 us (0.952)
  the two profiles are of different devices: /device:TPU:5 before, /device:TPU:23 now
where the time goes in v1:
time: 48.1 us; the launch traced here: 48 us
  Pallas kernels  46.3 us (96%)
  local copies, waits for them, and re-layouts  1.67 us (3%)
    pallas_call x1, Pallas kernels, planned_shards(): pl.pallas_call(functools.partial(planned, dims), out_shape=jax.ShapeDtype...  46.3 us
    unnamed x1, local copies, waits for them, and re-layouts  1.67 us

profile of v1, /device:TPU:23, one launch (start us, length us, event | category | flops | bytes accessed | tf_op | source)
XLA Modules:
  0.0 48.0 jit_solution(1551618803164350337)
XLA Ops:
  0.0 46.3 %shard_map.37 = f32[64,1024]{1,0:T(8,128)} custom-call(bf16[128,512]{1,0:T(8,128)(2,1)} %o_in.1, bf16[128,1024]{1,0:T(8,128)(2,1)} %b_in.1, bf16[128,2048]{1,0:T(8,128)(2,1)} %k_in.1), custom_call_target="tpu_custom_call" | custom-call | tf_op jit(solution)/shard_map/pallas_call | solution.py:620
  46.3 1.7 %copy.5 = f32[1024,64]{0,1:T(8,128)} copy(f32[1024,64]{0,1:T(8,128)} %bitcast.1) | data formatting | bytes 524288

commit v2 on v1

--- a/solution.py
+++ b/solution.py
@@ -373,7 +373,7 @@
         arrival[node, key] = now
         for child in kids[key].get(node, []):
             inward = (key[0] - node[0]) * (1 if 2 * node[0] < Z else -1)
-            rank = (key[2], -height[key][child], inward, key[1] == node[1])
+            rank = (2 * key[2] - height[key][child], key[2], inward, key[1] == node[1])
             queued.setdefault((node, child), []).append((rank, key))
 
     for key in sorted(parents):

time: 48.1 us -> 47.9 us (level)
  no operation moved by 1% of the time
where the time goes in v2:
time: 47.9 us; the launch traced here: 47.6 us
  Pallas kernels  45.9 us (96%)
  local copies, waits for them, and re-layouts  1.67 us (3%)
    pallas_call x1, Pallas kernels, planned_shards(): pl.pallas_call(functools.partial(planned, dims), out_shape=jax.ShapeDtype...  45.9 us
    unnamed x1, local copies, waits for them, and re-layouts  1.67 us

profile of v2, /device:TPU:23, one launch (start us, length us, event | category | flops | bytes accessed | tf_op | source)
XLA Modules:
  0.0 47.6 jit_solution(4110284944166818744)
XLA Ops:
  0.0 45.9 %shard_map.37 = f32[64,1024]{1,0:T(8,128)} custom-call(bf16[128,512]{1,0:T(8,128)(2,1)} %o_in.1, bf16[128,1024]{1,0:T(8,128)(2,1)} %b_in.1, bf16[128,2048]{1,0:T(8,128)(2,1)} %k_in.1), custom_call_target="tpu_custom_call" | custom-call | tf_op jit(solution)/shard_map/pallas_call | solution.py:620
  45.9 1.7 %copy.5 = f32[1024,64]{0,1:T(8,128)} copy(f32[1024,64]{0,1:T(8,128)} %bitcast.1) | data formatting | bytes 524288

commit v3 on v2

--- a/solution.py
+++ b/solution.py
@@ -373,7 +373,7 @@
         arrival[node, key] = now
         for child in kids[key].get(node, []):
             inward = (key[0] - node[0]) * (1 if 2 * node[0] < Z else -1)
-            rank = (2 * key[2] - height[key][child], key[2], inward, key[1] == node[1])
+            rank = (key[2], key[:2] == node, -height[key][child], inward, key[1] == node[1])
             queued.setdefault((node, child), []).append((rank, key))
 
     for key in sorted(parents):

time: 47.9 us -> 47.9 us (level)
  no operation moved by 1% of the time
where the time goes in v3:
time: 47.9 us; the launch traced here: 47.6 us
  Pallas kernels  45.9 us (96%)
  local copies, waits for them, and re-layouts  1.67 us (3%)
    pallas_call x1, Pallas kernels, planned_shards(): pl.pallas_call(functools.partial(planned, dims), out_shape=jax.ShapeDtype...  45.9 us
    unnamed x1, local copies, waits for them, and re-layouts  1.67 us

profile of v3, /device:TPU:23, one launch (start us, length us, event | category | flops | bytes accessed | tf_op | source)
XLA Modules:
  0.0 47.6 jit_solution(15241761355686724495)
XLA Ops:
  0.0 45.9 %shard_map.37 = f32[64,1024]{1,0:T(8,128)} custom-call(bf16[128,512]{1,0:T(8,128)(2,1)} %o_in.1, bf16[128,1024]{1,0:T(8,128)(2,1)} %b_in.1, bf16[128,2048]{1,0:T(8,128)(2,1)} %k_in.1), custom_call_target="tpu_custom_call" | custom-call | tf_op jit(solution)/shard_map/pallas_call | solution.py:620
  45.9 1.7 %copy.5 = f32[1024,64]{0,1:T(8,128)} copy(f32[1024,64]{0,1:T(8,128)} %bitcast.1) | data formatting | bytes 524288
